TPU v7x, 32 devices: a whole 2x2x4 slice. The times are simulated.
32 devices in a mesh: group: 2 (over y), section: 4 (over z), tensor: 4 (over x, core).
Axes of the slice: x: 2, y: 2, z: 4, core: 2. Of those that a mesh axis runs over, the one named last changes fastest.
Arguments:
- inputs: bfloat16 [48, 4096], P('group', 'tensor'), parts along dimension 0, may hold values from -6 to 6
- gains: float32 [4, 4096], P('section'), may hold values from 0.5 to 1.5
- w_query: bfloat16 [4, 4096, 4096], P('section', None, 'tensor'), may hold values from -0.09375 to 0.09375
- w_key: bfloat16 [4, 4096, 1024], P('section', None, 'tensor'), may hold values from -0.09375 to 0.09375
- w_value: bfloat16 [4, 4096, 1024], P('section', None, 'tensor'), may hold values from -0.09375 to 0.09375
- w_out: bfloat16 [4, 4096, 4096], P('section', 'tensor'), may hold values from -0.375 to 0.375
- key_cache: bfloat16 [4, 48, 128, 1024], P('section', 'group', None, 'tensor'), parts along dimension 1, may hold values from -64 to 64
- value_cache: bfloat16 [4, 48, 128, 1024], P('section', 'group', None, 'tensor'), parts along dimension 1, may hold values from -6 to 6
- cache_lens: int32 [48], P('group'), parts along dimension 0, may hold values from 1 to 128, as said below
- exit_plan: int32 [48], P('group'), parts along dimension 0, may hold values from 1 to 4, as said below
Outputs:
- section_hidden: bfloat16 [4, 48, 4096], P('section', 'group', 'tensor'), parts along dimension 1
- new_keys: bfloat16 [4, 48, 1024], P('section', 'group', 'tensor'), parts along dimension 1
- new_values: bfloat16 [4, 48, 1024], P('section', 'group', 'tensor'), parts along dimension 1
There are 2 independent parts, one for each index of `group`. A program takes and returns all parts, laid end to end along the dimension named above; an argument that names none is the same for every part. Nothing has to cross between parts.
Inputs may be any that keep to these rules, and one draw needn't show every extreme that they name: Cached slots 0 to cache_lens - 1 of a row are live; some row has exactly 128. `exit_plan`: some row runs all 4 layers in full.
All inputs are finite; a program needn't handle non-finite values.
Results may differ from a plain program's by a relative error of at most 0.022.
The roundings to bfloat16 on the way count: a program that leaves them out, or rounds other values in their place, can miss the bound.
Values may be sent and summed in bfloat16 or wider, within the bound.
A program may use at most 128 MiB of HBM per device.

v0:
```python
import math
import jax
import jax.numpy as jnp
from jax import lax
from jax.sharding import PartitionSpec as P

HEAD_DIM = 128
NORM_EPSILON = 1e-05
ROPE_BASE = 500000.0
MASKED_SCORE = -1e30


def shifted(value, axis, steps):
    count = lax.axis_size(axis)
    leading, last = (max(0, -steps), min(count, count - steps))
    return lax.ppermute(value, axis, [(source, source + steps) for source in range(leading, last)])


def rotate(vectors, positions):
    half_dim = vectors.shape[-1] // 2
    frequency = ROPE_BASE ** (-(jnp.arange(half_dim, dtype=jnp.float32) * 2.0 / vectors.shape[-1]))
    angles = positions.astype(jnp.float32)[:, None, None] * frequency[None, None, :]
    cos_part = jnp.cos(angles)
    sin_part = jnp.sin(angles)
    lower_half = vectors[..., :half_dim]
    upper_half = vectors[..., half_dim:]
    return jnp.concatenate(
        [
            lower_half * cos_part - upper_half * sin_part,
            upper_half * cos_part + lower_half * sin_part,
        ],
        axis=-1,
    )


def attend(
    normed, lengths, query_weight, key_weight, value_weight, keys_cached, values_cached, kv_local
):
    row_count = normed.shape[0]
    cache_slots = keys_cached.shape[1]
    per_kv = query_weight.shape[1] // (kv_local * HEAD_DIM)
    inv_root = 1.0 / math.sqrt(HEAD_DIM)
    queries = jnp.dot(normed, query_weight, preferred_element_type=jnp.float32).reshape(
        row_count, kv_local * per_kv, HEAD_DIM
    )
    queries = (
        rotate(queries, lengths).astype(jnp.bfloat16).reshape(row_count, kv_local, per_kv, HEAD_DIM)
    )
    key_new = jnp.dot(normed, key_weight, preferred_element_type=jnp.float32).reshape(
        row_count, kv_local, HEAD_DIM
    )
    key_new = rotate(key_new, lengths).astype(jnp.bfloat16)
    value_new = (
        jnp.dot(normed, value_weight, preferred_element_type=jnp.float32)
        .astype(jnp.bfloat16)
        .reshape(row_count, kv_local, HEAD_DIM)
    )
    keys_old = keys_cached.reshape(row_count, cache_slots, kv_local, HEAD_DIM)
    values_old = values_cached.reshape(row_count, cache_slots, kv_local, HEAD_DIM)
    visible = jnp.arange(cache_slots)[None, :] < lengths[:, None]
    scores_old = (
        jnp.einsum("rhgd,rlhd->rhgl", queries, keys_old, preferred_element_type=jnp.float32)
        * inv_root
    )
    scores_old = jnp.where(visible[:, None, None, :], scores_old, MASKED_SCORE)
    score_new = (
        jnp.einsum("rhgd,rhd->rhg", queries, key_new, preferred_element_type=jnp.float32) * inv_root
    )
    highest = jnp.maximum(jnp.max(scores_old, axis=-1), score_new)
    weight_old = jnp.exp(scores_old - highest[..., None])
    weight_new = jnp.exp(score_new - highest)
    denominator = jnp.sum(weight_old, axis=-1) + weight_new
    weight_old = (weight_old / denominator[..., None]).astype(jnp.bfloat16)
    weight_new = (weight_new / denominator).astype(jnp.bfloat16)
    attended = jnp.einsum(
        "rhgl,rlhd->rhgd", weight_old, values_old, preferred_element_type=jnp.float32
    )
    attended = (
        attended
        + weight_new.astype(jnp.float32)[..., None] * value_new.astype(jnp.float32)[:, :, None, :]
    )
    attended = attended.astype(jnp.bfloat16).reshape(row_count, kv_local * per_kv * HEAD_DIM)
    return (
        attended,
        key_new.reshape(row_count, kv_local * HEAD_DIM),
        value_new.reshape(row_count, kv_local * HEAD_DIM),
    )


def per_device(
    inputs, gains, w_query, w_key, w_value, w_out, key_cache, value_cache, cache_lens, exit_plan
):
    section_count = lax.axis_size("section")
    section_here = lax.axis_index("section")
    tensor_here = lax.axis_index("tensor")
    row_total = inputs.shape[0]
    shard_width = inputs.shape[1]
    kv_local = w_key.shape[2] // HEAD_DIM
    micro_count = 1
    block_rows = row_total // micro_count
    tick_count = section_count + micro_count - 1
    gain_row = gains[0]
    entering_all = lax.all_gather(inputs, "tensor", axis=1, tiled=True)
    carry_width = entering_all.shape[1]

    def advance(step_at, state_now):
        received, out_hidden, out_keys, out_values = state_now
        micro_at = step_at - section_here
        active = jnp.logical_and(micro_at >= 0, micro_at < micro_count)
        current = jnp.where(section_here == 0, entering_all, received)
        running = (section_here < exit_plan).astype(jnp.float32)[:, None]
        widened = current.astype(jnp.float32)
        normed = (
            widened
            * lax.rsqrt(jnp.mean(widened * widened, axis=-1, keepdims=True) + NORM_EPSILON)
            * gain_row[None, :]
        ).astype(jnp.bfloat16)
        keys_cached = key_cache[0]
        values_cached = value_cache[0]
        attended, key_new, value_new = attend(
            normed,
            cache_lens,
            w_query[0],
            w_key[0],
            w_value[0],
            keys_cached,
            values_cached,
            kv_local,
        )
        partial_value = jnp.dot(attended, w_out[0], preferred_element_type=jnp.float32)
        summed = lax.psum(partial_value, "tensor")
        following = (widened + running * summed).astype(jnp.bfloat16)
        own_piece = lax.dynamic_slice_in_dim(following, tensor_here * shard_width, shard_width, 1)
        passed = shifted(following, "section", 1)
        out_hidden = jnp.where(active, own_piece, out_hidden)
        out_keys = jnp.where(active, key_new, out_keys)
        out_values = jnp.where(active, value_new, out_values)
        return (passed, out_hidden, out_keys, out_values)

    initial = (
        jnp.zeros((block_rows, carry_width), jnp.bfloat16),
        jnp.zeros((row_total, shard_width), jnp.bfloat16),
        jnp.zeros((row_total, kv_local * HEAD_DIM), jnp.bfloat16),
        jnp.zeros((row_total, kv_local * HEAD_DIM), jnp.bfloat16),
    )
    final_state = lax.fori_loop(0, tick_count, advance, initial)
    return (final_state[1][None], final_state[2][None], final_state[3][None])


def solution(mesh):
    return jax.shard_map(
        per_device,
        mesh=mesh,
        in_specs=(
            P("group", "tensor"),
            P("section", None),
            P("section", None, "tensor"),
            P("section", None, "tensor"),
            P("section", None, "tensor"),
            P("section", "tensor", None),
            P("section", "group", None, "tensor"),
            P("section", "group", None, "tensor"),
            P("group"),
            P("group"),
        ),
        out_specs=(
            P("section", "group", "tensor"),
            P("section", "group", "tensor"),
            P("section", "group", "tensor"),
        ),
        check_vma=False,
    )
```

profile of v0, /device:TPU:0, one launch (start us, length us, event | category | flops | bytes accessed | tf_op | source)
XLA Modules:
  0.0 274.7 jit_solution(9247631473398930788)
XLA Ops:
  7.2 0.8 convert_bitcast_fusion
  8.0 7.0 %all_gather.3 = bf16[24,4096]{1,0:T(8,128)(2,1)S(1)} all-gather(bf16[24,1024]{1,0:T(8,128)(2,1)} %param.12), channel_id=1, replica_groups=mesh['group'=2,'section'=4,'tensor'=4] {'tensor'}, dimensions={1}, use_global_device_ids=true | all-gather | bytes 245760 | tf_op jit(solution)/shard_map/all_gather | solution.py:103
  15.0 3.5 %squeeze.67 = bf16[24,128,2,128]{3,2,1,0:T(2,128)(2,1)} reshape(bf16[1,24,128,256]{3,2,1,0:T(8,128)(2,1)} %param.18) | data formatting | bytes 3145728 | tf_op jit(solution)/shard_map/while/body/eval_jaxpr/reshape;while/body/eval_jaxpr/squeeze | solution.py:58
  18.5 1.9 squeeze.66
  20.4 2.9 %copy.25 = bf16[1,4096,256]{1,2,0:T(8,128)(2,1)S(1)} copy(bf16[1,4096,256]{2,1,0:T(8,128)(2,1)} %param.15) | data formatting | bytes 4194304
  23.3 11.4 %copy.24 = bf16[1,4096,1024]{1,2,0:T(8,128)(2,1)} copy(bf16[1,4096,1024]{2,1,0:T(8,128)(2,1)} %param.14) | data formatting | bytes 16777216
  34.7 232.8 %while.23 = (s32[]{:T(128)}, bf16[24,4096]{1,0:T(8,128)(2,1)S(1)}, bf16[24,1024]{1,0:T(8,128)(2,1)S(1)}, bf16[24,256]{1,0:T(8,128)(2,1)S(1)}, bf16[24,256]{1,0:T...) while((s32[]{:T(128)}, bf16[24,4096]{1,0:T(8,128)(2,1)S(1)}, ...), condition=%wide.wide.region_5.6_spmd.clone, body=%wide.wide.region_0.5_spmd.clone.sunk | while | flops 518737920 | bytes 52014272 | solution.py:146
  35.1 0.7 fusion.100
  35.8 0.9 copy-done
  37.2 5.8 %fusion.98 = f32[24,8,128]{2,0,1:T(8,128)S(1)} fusion(bf16[8,128,4096]{2,1,0:T(8,128)(2,1)} %bitcast.101, bf16[24,4096]{1,0:T(8,128)(2,1)S(1)} %get-tuple-element.801, f32[4096]{0:T(1024)S(1)} %bitcast.107, f32[24]{0:T(128)S(1)} %add_rsqrt_fusion.3), kind=kOutput, calls=%fused_computation.22.clone.clone.1 | convolution fusion | flops 201719808 | bytes 8700000 | tf_op jit(solution)/shard_map/while/body/eval_jaxpr/dot_general | solution.py:43
  43.7 1.1 fusion.99
  45.1 0.6 fusion.105
  45.7 5.3 %fusion.106 = f32[24,4096]{1,0:T(8,128)} fusion(bf16[24,1024]{1,0:T(8,128)(2,1)S(1)} %reshape.213, bf16[1,1024,4096]{2,1,0:T(8,128)(2,1)} %get-tuple-element.878), kind=kOutput, calls=%fused_computation.clone.clone.1 | convolution fusion | flops 201326592 | bytes 8830976 | tf_op jit(solution)/shard_map/while/body/eval_jaxpr/dot_general | solution.py:130
  51.2 34.2 %all-reduce.2.cloned.1.call-done = f32[24,4096]{1,0:T(8,128)} async-done(((f32[24,4096]{1,0:T(8,128)}), f32[24,4096]{1,0:T(8,128)}) %all-reduce.2.cloned.1.call-update) | async-done | bytes 393232 | tf_op jit(solution)/shard_map/while/body/eval_jaxpr/psum | solution.py:131
  85.3 1.1 fusion.107
  86.5 3.4 %collective-permute-start = (bf16[24,4096]{1,0:T(8,128)(2,1)S(1)}, bf16[24,4096]{1,0:T(8,128)(2,1)S(1)}, u32[]{:S(2)}, u32[]{:S(2)}) collective-permute-start(bf16[24,4096]{1,0:T(8,128)(2,1)S(1)} %fusion.107), channel_id=1, source_target_pairs={{0,4},{4,8},{8,12},{1,5},{5,9},{9,13},{2,6},{6,10},{10,14},{3,7},{... | collective-permute-start | bytes 589832 | tf_op jit(solution)/shard_map/while/body/eval_jaxpr/ppermute | solution.py:16
  89.9 3.1 %collective-permute-done = bf16[24,4096]{1,0:T(8,128)(2,1)S(1)} collective-permute-done((bf16[24,4096]{1,0:T(8,128)(2,1)S(1)}, bf16[24,4096]{1,0:T(8,128)(2,1)S(1)}, u32[]{:S(2)}, u32[]{:S(2)}) %collective-permute-start) | collective-permute-done | bytes 196640 | tf_op jit(solution)/shard_map/while/body/eval_jaxpr/ppermute | solution.py:16
  93.3 0.7 fusion.100
  94.0 0.9 copy-done
  95.4 5.8 %fusion.98 = f32[24,8,128]{2,0,1:T(8,128)S(1)} fusion(bf16[8,128,4096]{2,1,0:T(8,128)(2,1)} %bitcast.101, bf16[24,4096]{1,0:T(8,128)(2,1)S(1)} %get-tuple-element.801, f32[4096]{0:T(1024)S(1)} %bitcast.107, f32[24]{0:T(128)S(1)} %add_rsqrt_fusion.3), kind=kOutput, calls=%fused_computation.22.clone.clone.1 | convolution fusion | flops 201719808 | bytes 8700000 | tf_op jit(solution)/shard_map/while/body/eval_jaxpr/dot_general | solution.py:43
  101.9 1.1 fusion.99
  103.3 0.6 fusion.105
  103.9 5.3 %fusion.106 = f32[24,4096]{1,0:T(8,128)} fusion(bf16[24,1024]{1,0:T(8,128)(2,1)S(1)} %reshape.213, bf16[1,1024,4096]{2,1,0:T(8,128)(2,1)} %get-tuple-element.878), kind=kOutput, calls=%fused_computation.clone.clone.1 | convolution fusion | flops 201326592 | bytes 8830976 | tf_op jit(solution)/shard_map/while/body/eval_jaxpr/dot_general | solution.py:130
  109.4 34.1 %all-reduce.2.cloned.1.call-done = f32[24,4096]{1,0:T(8,128)} async-done(((f32[24,4096]{1,0:T(8,128)}), f32[24,4096]{1,0:T(8,128)}) %all-reduce.2.cloned.1.call-update) | async-done | bytes 393232 | tf_op jit(solution)/shard_map/while/body/eval_jaxpr/psum | solution.py:131
  143.5 1.1 fusion.107
  144.6 3.4 %collective-permute-start = (bf16[24,4096]{1,0:T(8,128)(2,1)S(1)}, bf16[24,4096]{1,0:T(8,128)(2,1)S(1)}, u32[]{:S(2)}, u32[]{:S(2)}) collective-permute-start(bf16[24,4096]{1,0:T(8,128)(2,1)S(1)} %fusion.107), channel_id=1, source_target_pairs={{0,4},{4,8},{8,12},{1,5},{5,9},{9,13},{2,6},{6,10},{10,14},{3,7},{... | collective-permute-start | bytes 589832 | tf_op jit(solution)/shard_map/while/body/eval_jaxpr/ppermute | solution.py:16
  148.1 3.1 %collective-permute-done = bf16[24,4096]{1,0:T(8,128)(2,1)S(1)} collective-permute-done((bf16[24,4096]{1,0:T(8,128)(2,1)S(1)}, bf16[24,4096]{1,0:T(8,128)(2,1)S(1)}, u32[]{:S(2)}, u32[]{:S(2)}) %collective-permute-start) | collective-permute-done | bytes 196640 | tf_op jit(solution)/shard_map/while/body/eval_jaxpr/ppermute | solution.py:16
  151.5 0.7 fusion.100
  152.2 0.9 copy-done
  153.6 5.8 %fusion.98 = f32[24,8,128]{2,0,1:T(8,128)S(1)} fusion(bf16[8,128,4096]{2,1,0:T(8,128)(2,1)} %bitcast.101, bf16[24,4096]{1,0:T(8,128)(2,1)S(1)} %get-tuple-element.801, f32[4096]{0:T(1024)S(1)} %bitcast.107, f32[24]{0:T(128)S(1)} %add_rsqrt_fusion.3), kind=kOutput, calls=%fused_computation.22.clone.clone.1 | convolution fusion | flops 201719808 | bytes 8700000 | tf_op jit(solution)/shard_map/while/body/eval_jaxpr/dot_general | solution.py:43
  160.1 1.1 fusion.99
  161.5 0.6 fusion.105
  162.1 5.3 %fusion.106 = f32[24,4096]{1,0:T(8,128)} fusion(bf16[24,1024]{1,0:T(8,128)(2,1)S(1)} %reshape.213, bf16[1,1024,4096]{2,1,0:T(8,128)(2,1)} %get-tuple-element.878), kind=kOutput, calls=%fused_computation.clone.clone.1 | convolution fusion | flops 201326592 | bytes 8830976 | tf_op jit(solution)/shard_map/while/body/eval_jaxpr/dot_general | solution.py:130
  167.6 34.1 %all-reduce.2.cloned.1.call-done = f32[24,4096]{1,0:T(8,128)} async-done(((f32[24,4096]{1,0:T(8,128)}), f32[24,4096]{1,0:T(8,128)}) %all-reduce.2.cloned.1.call-update) | async-done | bytes 393232 | tf_op jit(solution)/shard_map/while/body/eval_jaxpr/psum | solution.py:131
  201.7 1.1 fusion.107
  202.8 3.4 %collective-permute-start = (bf16[24,4096]{1,0:T(8,128)(2,1)S(1)}, bf16[24,4096]{1,0:T(8,128)(2,1)S(1)}, u32[]{:S(2)}, u32[]{:S(2)}) collective-permute-start(bf16[24,4096]{1,0:T(8,128)(2,1)S(1)} %fusion.107), channel_id=1, source_target_pairs={{0,4},{4,8},{8,12},{1,5},{5,9},{9,13},{2,6},{6,10},{10,14},{3,7},{... | collective-permute-start | bytes 589832 | tf_op jit(solution)/shard_map/while/body/eval_jaxpr/ppermute | solution.py:16
  206.2 3.1 %collective-permute-done = bf16[24,4096]{1,0:T(8,128)(2,1)S(1)} collective-permute-done((bf16[24,4096]{1,0:T(8,128)(2,1)S(1)}, bf16[24,4096]{1,0:T(8,128)(2,1)S(1)}, u32[]{:S(2)}, u32[]{:S(2)}) %collective-permute-start) | collective-permute-done | bytes 196640 | tf_op jit(solution)/shard_map/while/body/eval_jaxpr/ppermute | solution.py:16
  209.7 0.7 fusion.100
  210.3 0.9 copy-done
  211.7 5.8 %fusion.98 = f32[24,8,128]{2,0,1:T(8,128)S(1)} fusion(bf16[8,128,4096]{2,1,0:T(8,128)(2,1)} %bitcast.101, bf16[24,4096]{1,0:T(8,128)(2,1)S(1)} %get-tuple-element.801, f32[4096]{0:T(1024)S(1)} %bitcast.107, f32[24]{0:T(128)S(1)} %add_rsqrt_fusion.3), kind=kOutput, calls=%fused_computation.22.clone.clone.1 | convolution fusion | flops 201719808 | bytes 8700000 | tf_op jit(solution)/shard_map/while/body/eval_jaxpr/dot_general | solution.py:43
  218.2 1.1 fusion.99
  219.7 0.6 fusion.105
  220.3 5.3 %fusion.106 = f32[24,4096]{1,0:T(8,128)} fusion(bf16[24,1024]{1,0:T(8,128)(2,1)S(1)} %reshape.213, bf16[1,1024,4096]{2,1,0:T(8,128)(2,1)} %get-tuple-element.878), kind=kOutput, calls=%fused_computation.clone.clone.1 | convolution fusion | flops 201326592 | bytes 8830976 | tf_op jit(solution)/shard_map/while/body/eval_jaxpr/dot_general | solution.py:130
  225.7 34.1 %all-reduce.2.cloned.1.call-done = f32[24,4096]{1,0:T(8,128)} async-done(((f32[24,4096]{1,0:T(8,128)}), f32[24,4096]{1,0:T(8,128)}) %all-reduce.2.cloned.1.call-update) | async-done | bytes 393232 | tf_op jit(solution)/shard_map/while/body/eval_jaxpr/psum | solution.py:131
  259.8 1.1 fusion.107
  260.9 3.4 %collective-permute-start = (bf16[24,4096]{1,0:T(8,128)(2,1)S(1)}, bf16[24,4096]{1,0:T(8,128)(2,1)S(1)}, u32[]{:S(2)}, u32[]{:S(2)}) collective-permute-start(bf16[24,4096]{1,0:T(8,128)(2,1)S(1)} %fusion.107), channel_id=1, source_target_pairs={{0,4},{4,8},{8,12},{1,5},{5,9},{9,13},{2,6},{6,10},{10,14},{3,7},{... | collective-permute-start | bytes 589832 | tf_op jit(solution)/shard_map/while/body/eval_jaxpr/ppermute | solution.py:16
  264.4 3.1 %collective-permute-done = bf16[24,4096]{1,0:T(8,128)(2,1)S(1)} collective-permute-done((bf16[24,4096]{1,0:T(8,128)(2,1)S(1)}, bf16[24,4096]{1,0:T(8,128)(2,1)S(1)}, u32[]{:S(2)}, u32[]{:S(2)}) %collective-permute-start) | collective-permute-done | bytes 196640 | tf_op jit(solution)/shard_map/while/body/eval_jaxpr/ppermute | solution.py:16
  267.5 0.6 copy-done.5
  (125 shorter events, 7.8 us)
Async XLA Ops:
  7.2 11.3 %copy-start.2 = (bf16[1,24,128,256]{3,2,1,0:T(8,128)(2,1)S(1)}, bf16[1,24,128,256]{3,2,1,0:T(8,128)(2,1)}, u32[]{:S(2)}) copy-start(bf16[1,24,128,256]{3,2,1,0:T(8,128)(2,1)} %param.19) | copy-start | bytes 4718596
  23.3 11.4 %copy-start.1 = (f32[1,4096]{1,0:T(1,128)S(1)}, f32[1,4096]{1,0:T(1,128)}, u32[]{:S(2)}) copy-start(f32[1,4096]{1,0:T(1,128)} %param.13) | copy-start | bytes 49156
  23.3 11.4 %copy-start.8 = (s32[24]{0:T(128)S(1)}, s32[24]{0:T(128)}, u32[]{:S(2)}) copy-start(s32[24]{0:T(128)} %param.20) | copy-start | bytes 292
  23.3 11.4 %copy-start.9 = (s32[24]{0:T(128)S(1)}, s32[24]{0:T(128)}, u32[]{:S(2)}) copy-start(s32[24]{0:T(128)} %param.21) | copy-start | bytes 292
  34.8 50.6 %all-reduce.2.cloned.1.call-start = ((), (), s32[]{:S(2)}) async-start(), calls=%async_computation | async-start | bytes 786432 | tf_op jit(solution)/shard_map/while/body/eval_jaxpr/psum | solution.py:131
  35.1 1.6 copy-start
  37.2 6.5 %copy-start.3 = (bf16[24,128,2,128]{3,2,1,0:T(2,128)(2,1)S(1)}, bf16[24,128,2,128]{3,2,1,0:T(2,128)(2,1)}, u32[]{:S(2)}) copy-start(bf16[24,128,2,128]{3,2,1,0:T(2,128)(2,1)} %get-tuple-element.881) | copy-start | bytes 4718596 | tf_op jit(solution)/shard_map/while
  43.0 2.1 copy-start.4
  86.5 6.6 %collective-permute-start = (bf16[24,4096]{1,0:T(8,128)(2,1)S(1)}, bf16[24,4096]{1,0:T(8,128)(2,1)S(1)}, u32[]{:S(2)}, u32[]{:S(2)}) collective-permute-start(bf16[24,4096]{1,0:T(8,128)(2,1)S(1)} %fusion.107), channel_id=1, source_target_pairs={{0,4},{4,8},{8,12},{1,5},{5,9},{9,13},{2,6},{6,10},{10,14},{3,7},{... | collective-permute-start | bytes 589832 | tf_op jit(solution)/shard_map/while/body/eval_jaxpr/ppermute | solution.py:16
  93.0 50.5 %all-reduce.2.cloned.1.call-start = ((), (), s32[]{:S(2)}) async-start(), calls=%async_computation | async-start | bytes 786432 | tf_op jit(solution)/shard_map/while/body/eval_jaxpr/psum | solution.py:131
  93.3 1.6 copy-start
  95.4 6.5 %copy-start.3 = (bf16[24,128,2,128]{3,2,1,0:T(2,128)(2,1)S(1)}, bf16[24,128,2,128]{3,2,1,0:T(2,128)(2,1)}, u32[]{:S(2)}) copy-start(bf16[24,128,2,128]{3,2,1,0:T(2,128)(2,1)} %get-tuple-element.881) | copy-start | bytes 4718596 | tf_op jit(solution)/shard_map/while
  101.2 2.1 copy-start.4
  144.6 6.6 %collective-permute-start = (bf16[24,4096]{1,0:T(8,128)(2,1)S(1)}, bf16[24,4096]{1,0:T(8,128)(2,1)S(1)}, u32[]{:S(2)}, u32[]{:S(2)}) collective-permute-start(bf16[24,4096]{1,0:T(8,128)(2,1)S(1)} %fusion.107), channel_id=1, source_target_pairs={{0,4},{4,8},{8,12},{1,5},{5,9},{9,13},{2,6},{6,10},{10,14},{3,7},{... | collective-permute-start | bytes 589832 | tf_op jit(solution)/shard_map/while/body/eval_jaxpr/ppermute | solution.py:16
  151.2 50.5 %all-reduce.2.cloned.1.call-start = ((), (), s32[]{:S(2)}) async-start(), calls=%async_computation | async-start | bytes 786432 | tf_op jit(solution)/shard_map/while/body/eval_jaxpr/psum | solution.py:131
  151.5 1.6 copy-start
  153.6 6.5 %copy-start.3 = (bf16[24,128,2,128]{3,2,1,0:T(2,128)(2,1)S(1)}, bf16[24,128,2,128]{3,2,1,0:T(2,128)(2,1)}, u32[]{:S(2)}) copy-start(bf16[24,128,2,128]{3,2,1,0:T(2,128)(2,1)} %get-tuple-element.881) | copy-start | bytes 4718596 | tf_op jit(solution)/shard_map/while
  159.3 2.1 copy-start.4
  202.8 6.6 %collective-permute-start = (bf16[24,4096]{1,0:T(8,128)(2,1)S(1)}, bf16[24,4096]{1,0:T(8,128)(2,1)S(1)}, u32[]{:S(2)}, u32[]{:S(2)}) collective-permute-start(bf16[24,4096]{1,0:T(8,128)(2,1)S(1)} %fusion.107), channel_id=1, source_target_pairs={{0,4},{4,8},{8,12},{1,5},{5,9},{9,13},{2,6},{6,10},{10,14},{3,7},{... | collective-permute-start | bytes 589832 | tf_op jit(solution)/shard_map/while/body/eval_jaxpr/ppermute | solution.py:16
  209.3 50.5 %all-reduce.2.cloned.1.call-start = ((), (), s32[]{:S(2)}) async-start(), calls=%async_computation | async-start | bytes 786432 | tf_op jit(solution)/shard_map/while/body/eval_jaxpr/psum | solution.py:131
  209.6 1.6 copy-start
  211.7 6.5 %copy-start.3 = (bf16[24,128,2,128]{3,2,1,0:T(2,128)(2,1)S(1)}, bf16[24,128,2,128]{3,2,1,0:T(2,128)(2,1)}, u32[]{:S(2)}) copy-start(bf16[24,128,2,128]{3,2,1,0:T(2,128)(2,1)} %get-tuple-element.881) | copy-start | bytes 4718596 | tf_op jit(solution)/shard_map/while
  217.5 2.1 copy-start.4
  260.9 6.6 %collective-permute-start = (bf16[24,4096]{1,0:T(8,128)(2,1)S(1)}, bf16[24,4096]{1,0:T(8,128)(2,1)S(1)}, u32[]{:S(2)}, u32[]{:S(2)}) collective-permute-start(bf16[24,4096]{1,0:T(8,128)(2,1)S(1)} %fusion.107), channel_id=1, source_target_pairs={{0,4},{4,8},{8,12},{1,5},{5,9},{9,13},{2,6},{6,10},{10,14},{3,7},{... | collective-permute-start | bytes 589832 | tf_op jit(solution)/shard_map/while/body/eval_jaxpr/ppermute | solution.py:16
  267.5 0.6 copy-start.5
  267.5 0.6 copy-start.6
  267.5 0.6 copy-start.7
Sparse Core Ops, SparseCore 0:
  51.2 34.0 all-reduce.1
  109.4 34.0 all-reduce.1
  167.6 34.0 all-reduce.1
  225.8 34.0 all-reduce.1
where the time goes:
time: 276 us; the launch traced here: 275 us
  waiting for transfers between devices  149 us (54%)
  matrix products  56.4 us (20%)
  local copies, waits for them, and re-layouts  24.5 us (9%)
  between operations  13.8 us (5%)
  starting transfers between devices  13.7 us (5%)
  other arithmetic  9.68 us (4%)
  blocking collectives  7.03 us (3%)
    psum x4, waiting for transfers between devices, advance(): summed = lax.psum(partial_value, 'tensor')  136 us
    dot_general x4, matrix products, attend(): jnp.dot(normed, query_weight, preferred_element_type=jnp.float32)  23.1 us
    dot_general x4, matrix products, advance(): jnp.dot(attended, w_out[0], preferred_element_type=jnp.float32)  21.3 us
    unnamed x16, local copies, waits for them, and re-layouts  14.9 us
    ppermute x4, starting transfers between devices, shifted(): lax.ppermute(value, axis, [(source, source + steps) for source in range(l...  13.6 us
    ppermute x4, waiting for transfers between devices, shifted(): lax.ppermute(value, axis, [(source, source + steps) for source in range(l...  12.5 us
    all_gather x1, blocking collectives, per_device(): entering_all = lax.all_gather(inputs, 'tensor', axis=1, tiled=True)  7.03 us
  transfers between devices with their start and end apart: 8, of which 8 were waited for; matrix products, arithmetic and copies ran while one was open for 0% of the time, Pallas kernels for 0%

commit v1 on v0

--- a/solution.py
+++ b/solution.py
@@ -128,7 +128,7 @@
             kv_local,
         )
         partial_value = jnp.dot(attended, w_out[0], preferred_element_type=jnp.float32)
-        summed = lax.psum(partial_value, "tensor")
+        summed = lax.all_gather(partial_value, axis_name="tensor").sum(axis=0)
         following = (widened + running * summed).astype(jnp.bfloat16)
         own_piece = lax.dynamic_slice_in_dim(following, tensor_here * shard_width, shard_width, 1)
         passed = shifted(following, "section", 1)

time: 276 us -> 230 us (0.83)
  waiting for transfers between devices: 149 us -> 101 us
    psum x4 -> x0, waiting for transfers between devices: 136 us -> none  [advance(): summed = lax.psum(partial_value, 'tensor')]
    all_gather x0 -> x4, waiting for transfers between devices: none -> 83.4 us  [advance(): summed = lax.all_gather(partial_value, axis_name='tensor').sum(axis=0)]
    reduce_sum x0 -> x4, other arithmetic: none -> 6.13 us  [advance(): summed = lax.all_gather(partial_value, axis_name='tensor').sum(axis=0)]
    ppermute x4, waiting for transfers between devices: 12.5 us -> 18 us  [shifted(): lax.ppermute(value, axis, [(source, source + steps) for source in range(l...]
    convert_element_type x4, other arithmetic: 4.44 us -> 0.47 us  [advance(): following = (widened + running * summed).astype(jnp.bfloat16)]
where the time goes in v1:
time: 230 us; the launch traced here: 229 us
  waiting for transfers between devices  101 us (44%)
  matrix products  56.5 us (25%)
  local copies, waits for them, and re-layouts  24.5 us (11%)
  between operations  13.8 us (6%)
  starting transfers between devices  13.7 us (6%)
  other arithmetic  11.8 us (5%)
  blocking collectives  7.03 us (3%)
    all_gather x4, waiting for transfers between devices, advance(): summed = lax.all_gather(partial_value, axis_name='tensor').sum(axis=0)  83.4 us
    dot_general x4, matrix products, attend(): jnp.dot(normed, query_weight, preferred_element_type=jnp.float32)  23.1 us
    dot_general x4, matrix products, advance(): jnp.dot(attended, w_out[0], preferred_element_type=jnp.float32)  21.5 us
    ppermute x4, waiting for transfers between devices, shifted(): lax.ppermute(value, axis, [(source, source + steps) for source in range(l...  18 us
    unnamed x16, local copies, waits for them, and re-layouts  14.9 us
    ppermute x4, starting transfers between devices, shifted(): lax.ppermute(value, axis, [(source, source + steps) for source in range(l...  13.6 us
    all_gather x1, blocking collectives, per_device(): entering_all = lax.all_gather(inputs, 'tensor', axis=1, tiled=True)  7.03 us
    reduce_sum x4, other arithmetic, advance(): summed = lax.all_gather(partial_value, axis_name='tensor').sum(axis=0)  6.13 us
  transfers between devices with their start and end apart: 8, of which 8 were waited for; matrix products, arithmetic and copies ran while one was open for 0% of the time, Pallas kernels for 0%

profile of v1, /device:TPU:0, one launch (start us, length us, event | category | flops | bytes accessed | tf_op | source)
XLA Modules:
  0.0 229.4 jit_solution(15585385983247868905)
XLA Ops:
  7.2 0.8 convert_bitcast_fusion
  8.0 7.0 %all_gather.23 = bf16[24,4096]{1,0:T(8,128)(2,1)S(1)} all-gather(bf16[24,1024]{1,0:T(8,128)(2,1)} %param.12), channel_id=1, replica_groups=mesh['group'=2,'section'=4,'tensor'=4] {'tensor'}, dimensions={1}, use_global_device_ids=true | all-gather | bytes 245760 | tf_op jit(solution)/shard_map/all_gather | solution.py:103
  15.0 3.5 %squeeze.67 = bf16[24,128,2,128]{3,2,1,0:T(2,128)(2,1)} reshape(bf16[1,24,128,256]{3,2,1,0:T(8,128)(2,1)} %param.18) | data formatting | bytes 3145728 | tf_op jit(solution)/shard_map/while/body/eval_jaxpr/reshape;while/body/eval_jaxpr/squeeze | solution.py:58
  18.5 1.9 squeeze.66
  20.4 2.9 %copy.25 = bf16[1,4096,256]{1,2,0:T(8,128)(2,1)S(1)} copy(bf16[1,4096,256]{2,1,0:T(8,128)(2,1)} %param.15) | data formatting | bytes 4194304
  23.3 11.4 %copy.24 = bf16[1,4096,1024]{1,2,0:T(8,128)(2,1)} copy(bf16[1,4096,1024]{2,1,0:T(8,128)(2,1)} %param.14) | data formatting | bytes 16777216
  34.8 187.5 %while.23 = (s32[]{:T(128)}, bf16[24,4096]{1,0:T(8,128)(2,1)S(1)}, bf16[24,1024]{1,0:T(8,128)(2,1)S(1)}, bf16[24,256]{1,0:T(8,128)(2,1)S(1)}, bf16[24,256]{1,0:T...) while((s32[]{:T(128)}, bf16[24,4096]{1,0:T(8,128)(2,1)S(1)}, ...), condition=%wide.wide.region_5.6_spmd.clone, body=%wide.wide.region_0.5_spmd.clone.sunk | while | flops 518934528 | bytes 57519312 | solution.py:146
  35.1 0.7 fusion.100
  35.8 0.9 copy-done
  37.2 5.8 %fusion.98 = f32[24,8,128]{2,0,1:T(8,128)S(1)} fusion(bf16[8,128,4096]{2,1,0:T(8,128)(2,1)} %bitcast.105, bf16[24,4096]{1,0:T(8,128)(2,1)S(1)} %get-tuple-element.801, f32[4096]{0:T(1024)S(1)} %bitcast.112, f32[24]{0:T(128)S(1)} %add_rsqrt_fusion.3), kind=kOutput, calls=%fused_computation.22.clone.clone.1 | convolution fusion | flops 201719808 | bytes 8700000 | tf_op jit(solution)/shard_map/while/body/eval_jaxpr/dot_general | solution.py:43
  43.7 1.1 fusion.99
  45.1 0.6 fusion.105
  45.7 5.4 %fusion.106 = f32[24,4096]{1,0:T(8,128)} fusion(bf16[24,1024]{1,0:T(8,128)(2,1)S(1)} %reshape.215, bf16[1,1024,4096]{2,1,0:T(8,128)(2,1)} %get-tuple-element.880), kind=kOutput, calls=%fused_computation.clone.clone.1 | convolution fusion | flops 201326592 | bytes 8830976 | tf_op jit(solution)/shard_map/while/body/eval_jaxpr/dot_general | solution.py:130
  51.2 21.2 %all-gather.7.cloned.1.call-done = f32[96,4096]{1,0:T(8,128)} async-done(((f32[24,4096]{1,0:T(8,128)}), f32[96,4096]{1,0:T(8,128)}) %all-gather.7.cloned.1.call-update) | async-done | bytes 1572880 | tf_op jit(solution)/shard_map/while/body/eval_jaxpr/all_gather | solution.py:131
  72.4 1.5 reduce_sum.61
  74.1 3.4 %collective-permute-start = (bf16[24,4096]{1,0:T(8,128)(2,1)S(1)}, bf16[24,4096]{1,0:T(8,128)(2,1)S(1)}, u32[]{:S(2)}, u32[]{:S(2)}) collective-permute-start(bf16[24,4096]{1,0:T(8,128)(2,1)S(1)} %fusion.107), channel_id=1, source_target_pairs={{0,4},{4,8},{8,12},{1,5},{5,9},{9,13},{2,6},{6,10},{10,14},{3,7},{... | collective-permute-start | bytes 589832 | tf_op jit(solution)/shard_map/while/body/eval_jaxpr/ppermute | solution.py:16
  77.5 4.5 %collective-permute-done = bf16[24,4096]{1,0:T(8,128)(2,1)S(1)} collective-permute-done((bf16[24,4096]{1,0:T(8,128)(2,1)S(1)}, bf16[24,4096]{1,0:T(8,128)(2,1)S(1)}, u32[]{:S(2)}, u32[]{:S(2)}) %collective-permute-start) | collective-permute-done | bytes 196640 | tf_op jit(solution)/shard_map/while/body/eval_jaxpr/ppermute | solution.py:16
  82.3 0.7 fusion.100
  83.0 0.9 copy-done
  84.4 5.8 %fusion.98 = f32[24,8,128]{2,0,1:T(8,128)S(1)} fusion(bf16[8,128,4096]{2,1,0:T(8,128)(2,1)} %bitcast.105, bf16[24,4096]{1,0:T(8,128)(2,1)S(1)} %get-tuple-element.801, f32[4096]{0:T(1024)S(1)} %bitcast.112, f32[24]{0:T(128)S(1)} %add_rsqrt_fusion.3), kind=kOutput, calls=%fused_computation.22.clone.clone.1 | convolution fusion | flops 201719808 | bytes 8700000 | tf_op jit(solution)/shard_map/while/body/eval_jaxpr/dot_general | solution.py:43
  90.9 1.1 fusion.99
  92.3 0.6 fusion.105
  93.0 5.4 %fusion.106 = f32[24,4096]{1,0:T(8,128)} fusion(bf16[24,1024]{1,0:T(8,128)(2,1)S(1)} %reshape.215, bf16[1,1024,4096]{2,1,0:T(8,128)(2,1)} %get-tuple-element.880), kind=kOutput, calls=%fused_computation.clone.clone.1 | convolution fusion | flops 201326592 | bytes 8830976 | tf_op jit(solution)/shard_map/while/body/eval_jaxpr/dot_general | solution.py:130
  98.5 20.7 %all-gather.7.cloned.1.call-done = f32[96,4096]{1,0:T(8,128)} async-done(((f32[24,4096]{1,0:T(8,128)}), f32[96,4096]{1,0:T(8,128)}) %all-gather.7.cloned.1.call-update) | async-done | bytes 1572880 | tf_op jit(solution)/shard_map/while/body/eval_jaxpr/all_gather | solution.py:131
  119.2 1.5 reduce_sum.61
  120.8 3.4 %collective-permute-start = (bf16[24,4096]{1,0:T(8,128)(2,1)S(1)}, bf16[24,4096]{1,0:T(8,128)(2,1)S(1)}, u32[]{:S(2)}, u32[]{:S(2)}) collective-permute-start(bf16[24,4096]{1,0:T(8,128)(2,1)S(1)} %fusion.107), channel_id=1, source_target_pairs={{0,4},{4,8},{8,12},{1,5},{5,9},{9,13},{2,6},{6,10},{10,14},{3,7},{... | collective-permute-start | bytes 589832 | tf_op jit(solution)/shard_map/while/body/eval_jaxpr/ppermute | solution.py:16
  124.3 4.5 %collective-permute-done = bf16[24,4096]{1,0:T(8,128)(2,1)S(1)} collective-permute-done((bf16[24,4096]{1,0:T(8,128)(2,1)S(1)}, bf16[24,4096]{1,0:T(8,128)(2,1)S(1)}, u32[]{:S(2)}, u32[]{:S(2)}) %collective-permute-start) | collective-permute-done | bytes 196640 | tf_op jit(solution)/shard_map/while/body/eval_jaxpr/ppermute | solution.py:16
  129.1 0.7 fusion.100
  129.7 0.9 copy-done
  131.1 5.8 %fusion.98 = f32[24,8,128]{2,0,1:T(8,128)S(1)} fusion(bf16[8,128,4096]{2,1,0:T(8,128)(2,1)} %bitcast.105, bf16[24,4096]{1,0:T(8,128)(2,1)S(1)} %get-tuple-element.801, f32[4096]{0:T(1024)S(1)} %bitcast.112, f32[24]{0:T(128)S(1)} %add_rsqrt_fusion.3), kind=kOutput, calls=%fused_computation.22.clone.clone.1 | convolution fusion | flops 201719808 | bytes 8700000 | tf_op jit(solution)/shard_map/while/body/eval_jaxpr/dot_general | solution.py:43
  137.7 1.1 fusion.99
  139.1 0.6 fusion.105
  139.7 5.4 %fusion.106 = f32[24,4096]{1,0:T(8,128)} fusion(bf16[24,1024]{1,0:T(8,128)(2,1)S(1)} %reshape.215, bf16[1,1024,4096]{2,1,0:T(8,128)(2,1)} %get-tuple-element.880), kind=kOutput, calls=%fused_computation.clone.clone.1 | convolution fusion | flops 201326592 | bytes 8830976 | tf_op jit(solution)/shard_map/while/body/eval_jaxpr/dot_general | solution.py:130
  145.2 20.7 %all-gather.7.cloned.1.call-done = f32[96,4096]{1,0:T(8,128)} async-done(((f32[24,4096]{1,0:T(8,128)}), f32[96,4096]{1,0:T(8,128)}) %all-gather.7.cloned.1.call-update) | async-done | bytes 1572880 | tf_op jit(solution)/shard_map/while/body/eval_jaxpr/all_gather | solution.py:131
  165.9 1.5 reduce_sum.61
  167.6 3.4 %collective-permute-start = (bf16[24,4096]{1,0:T(8,128)(2,1)S(1)}, bf16[24,4096]{1,0:T(8,128)(2,1)S(1)}, u32[]{:S(2)}, u32[]{:S(2)}) collective-permute-start(bf16[24,4096]{1,0:T(8,128)(2,1)S(1)} %fusion.107), channel_id=1, source_target_pairs={{0,4},{4,8},{8,12},{1,5},{5,9},{9,13},{2,6},{6,10},{10,14},{3,7},{... | collective-permute-start | bytes 589832 | tf_op jit(solution)/shard_map/while/body/eval_jaxpr/ppermute | solution.py:16
  171.0 4.5 %collective-permute-done = bf16[24,4096]{1,0:T(8,128)(2,1)S(1)} collective-permute-done((bf16[24,4096]{1,0:T(8,128)(2,1)S(1)}, bf16[24,4096]{1,0:T(8,128)(2,1)S(1)}, u32[]{:S(2)}, u32[]{:S(2)}) %collective-permute-start) | collective-permute-done | bytes 196640 | tf_op jit(solution)/shard_map/while/body/eval_jaxpr/ppermute | solution.py:16
  175.8 0.7 fusion.100
  176.5 0.9 copy-done
  177.9 5.8 %fusion.98 = f32[24,8,128]{2,0,1:T(8,128)S(1)} fusion(bf16[8,128,4096]{2,1,0:T(8,128)(2,1)} %bitcast.105, bf16[24,4096]{1,0:T(8,128)(2,1)S(1)} %get-tuple-element.801, f32[4096]{0:T(1024)S(1)} %bitcast.112, f32[24]{0:T(128)S(1)} %add_rsqrt_fusion.3), kind=kOutput, calls=%fused_computation.22.clone.clone.1 | convolution fusion | flops 201719808 | bytes 8700000 | tf_op jit(solution)/shard_map/while/body/eval_jaxpr/dot_general | solution.py:43
  184.4 1.1 fusion.99
  185.8 0.6 fusion.105
  186.4 5.4 %fusion.106 = f32[24,4096]{1,0:T(8,128)} fusion(bf16[24,1024]{1,0:T(8,128)(2,1)S(1)} %reshape.215, bf16[1,1024,4096]{2,1,0:T(8,128)(2,1)} %get-tuple-element.880), kind=kOutput, calls=%fused_computation.clone.clone.1 | convolution fusion | flops 201326592 | bytes 8830976 | tf_op jit(solution)/shard_map/while/body/eval_jaxpr/dot_general | solution.py:130
  191.9 20.7 %all-gather.7.cloned.1.call-done = f32[96,4096]{1,0:T(8,128)} async-done(((f32[24,4096]{1,0:T(8,128)}), f32[96,4096]{1,0:T(8,128)}) %all-gather.7.cloned.1.call-update) | async-done | bytes 1572880 | tf_op jit(solution)/shard_map/while/body/eval_jaxpr/all_gather | solution.py:131
  212.6 1.5 reduce_sum.61
  214.3 3.4 %collective-permute-start = (bf16[24,4096]{1,0:T(8,128)(2,1)S(1)}, bf16[24,4096]{1,0:T(8,128)(2,1)S(1)}, u32[]{:S(2)}, u32[]{:S(2)}) collective-permute-start(bf16[24,4096]{1,0:T(8,128)(2,1)S(1)} %fusion.107), channel_id=1, source_target_pairs={{0,4},{4,8},{8,12},{1,5},{5,9},{9,13},{2,6},{6,10},{10,14},{3,7},{... | collective-permute-start | bytes 589832 | tf_op jit(solution)/shard_map/while/body/eval_jaxpr/ppermute | solution.py:16
  217.7 4.5 %collective-permute-done = bf16[24,4096]{1,0:T(8,128)(2,1)S(1)} collective-permute-done((bf16[24,4096]{1,0:T(8,128)(2,1)S(1)}, bf16[24,4096]{1,0:T(8,128)(2,1)S(1)}, u32[]{:S(2)}, u32[]{:S(2)}) %collective-permute-start) | collective-permute-done | bytes 196640 | tf_op jit(solution)/shard_map/while/body/eval_jaxpr/ppermute | solution.py:16
  222.2 0.6 copy-done.5
  (129 shorter events, 8.3 us)
Async XLA Ops:
  7.2 11.3 %copy-start.2 = (bf16[1,24,128,256]{3,2,1,0:T(8,128)(2,1)S(1)}, bf16[1,24,128,256]{3,2,1,0:T(8,128)(2,1)}, u32[]{:S(2)}) copy-start(bf16[1,24,128,256]{3,2,1,0:T(8,128)(2,1)} %param.19) | copy-start | bytes 4718596
  23.3 11.4 %copy-start.1 = (f32[1,4096]{1,0:T(1,128)S(1)}, f32[1,4096]{1,0:T(1,128)}, u32[]{:S(2)}) copy-start(f32[1,4096]{1,0:T(1,128)} %param.13) | copy-start | bytes 49156
  23.3 11.4 %copy-start.8 = (s32[24]{0:T(128)S(1)}, s32[24]{0:T(128)}, u32[]{:S(2)}) copy-start(s32[24]{0:T(128)} %param.20) | copy-start | bytes 292
  23.3 11.4 %copy-start.9 = (s32[24]{0:T(128)S(1)}, s32[24]{0:T(128)}, u32[]{:S(2)}) copy-start(s32[24]{0:T(128)} %param.21) | copy-start | bytes 292
  34.8 37.7 %all-gather.7.cloned.1.call-start = ((), (), s32[]{:S(2)}) async-start(), calls=%async_computation | async-start | bytes 1966080 | tf_op jit(solution)/shard_map/while/body/eval_jaxpr/all_gather | solution.py:131
  35.1 1.6 copy-start
  37.2 6.5 %copy-start.3 = (bf16[24,128,2,128]{3,2,1,0:T(2,128)(2,1)S(1)}, bf16[24,128,2,128]{3,2,1,0:T(2,128)(2,1)}, u32[]{:S(2)}) copy-start(bf16[24,128,2,128]{3,2,1,0:T(2,128)(2,1)} %get-tuple-element.883) | copy-start | bytes 4718596 | tf_op jit(solution)/shard_map/while
  43.0 2.1 copy-start.4
  74.1 7.9 %collective-permute-start = (bf16[24,4096]{1,0:T(8,128)(2,1)S(1)}, bf16[24,4096]{1,0:T(8,128)(2,1)S(1)}, u32[]{:S(2)}, u32[]{:S(2)}) collective-permute-start(bf16[24,4096]{1,0:T(8,128)(2,1)S(1)} %fusion.107), channel_id=1, source_target_pairs={{0,4},{4,8},{8,12},{1,5},{5,9},{9,13},{2,6},{6,10},{10,14},{3,7},{... | collective-permute-start | bytes 589832 | tf_op jit(solution)/shard_map/while/body/eval_jaxpr/ppermute | solution.py:16
  82.0 37.1 %all-gather.7.cloned.1.call-start = ((), (), s32[]{:S(2)}) async-start(), calls=%async_computation | async-start | bytes 1966080 | tf_op jit(solution)/shard_map/while/body/eval_jaxpr/all_gather | solution.py:131
  82.3 1.6 copy-start
  84.4 6.5 %copy-start.3 = (bf16[24,128,2,128]{3,2,1,0:T(2,128)(2,1)S(1)}, bf16[24,128,2,128]{3,2,1,0:T(2,128)(2,1)}, u32[]{:S(2)}) copy-start(bf16[24,128,2,128]{3,2,1,0:T(2,128)(2,1)} %get-tuple-element.883) | copy-start | bytes 4718596 | tf_op jit(solution)/shard_map/while
  90.2 2.1 copy-start.4
  120.8 7.9 %collective-permute-start = (bf16[24,4096]{1,0:T(8,128)(2,1)S(1)}, bf16[24,4096]{1,0:T(8,128)(2,1)S(1)}, u32[]{:S(2)}, u32[]{:S(2)}) collective-permute-start(bf16[24,4096]{1,0:T(8,128)(2,1)S(1)} %fusion.107), channel_id=1, source_target_pairs={{0,4},{4,8},{8,12},{1,5},{5,9},{9,13},{2,6},{6,10},{10,14},{3,7},{... | collective-permute-start | bytes 589832 | tf_op jit(solution)/shard_map/while/body/eval_jaxpr/ppermute | solution.py:16
  128.8 37.1 %all-gather.7.cloned.1.call-start = ((), (), s32[]{:S(2)}) async-start(), calls=%async_computation | async-start | bytes 1966080 | tf_op jit(solution)/shard_map/while/body/eval_jaxpr/all_gather | solution.py:131
  129.1 1.6 copy-start
  131.1 6.5 %copy-start.3 = (bf16[24,128,2,128]{3,2,1,0:T(2,128)(2,1)S(1)}, bf16[24,128,2,128]{3,2,1,0:T(2,128)(2,1)}, u32[]{:S(2)}) copy-start(bf16[24,128,2,128]{3,2,1,0:T(2,128)(2,1)} %get-tuple-element.883) | copy-start | bytes 4718596 | tf_op jit(solution)/shard_map/while
  136.9 2.1 copy-start.4
  167.6 7.9 %collective-permute-start = (bf16[24,4096]{1,0:T(8,128)(2,1)S(1)}, bf16[24,4096]{1,0:T(8,128)(2,1)S(1)}, u32[]{:S(2)}, u32[]{:S(2)}) collective-permute-start(bf16[24,4096]{1,0:T(8,128)(2,1)S(1)} %fusion.107), channel_id=1, source_target_pairs={{0,4},{4,8},{8,12},{1,5},{5,9},{9,13},{2,6},{6,10},{10,14},{3,7},{... | collective-permute-start | bytes 589832 | tf_op jit(solution)/shard_map/while/body/eval_jaxpr/ppermute | solution.py:16
  175.5 37.1 %all-gather.7.cloned.1.call-start = ((), (), s32[]{:S(2)}) async-start(), calls=%async_computation | async-start | bytes 1966080 | tf_op jit(solution)/shard_map/while/body/eval_jaxpr/all_gather | solution.py:131
  175.8 1.6 copy-start
  177.9 6.5 %copy-start.3 = (bf16[24,128,2,128]{3,2,1,0:T(2,128)(2,1)S(1)}, bf16[24,128,2,128]{3,2,1,0:T(2,128)(2,1)}, u32[]{:S(2)}) copy-start(bf16[24,128,2,128]{3,2,1,0:T(2,128)(2,1)} %get-tuple-element.883) | copy-start | bytes 4718596 | tf_op jit(solution)/shard_map/while
  183.7 2.1 copy-start.4
  214.3 7.9 %collective-permute-start = (bf16[24,4096]{1,0:T(8,128)(2,1)S(1)}, bf16[24,4096]{1,0:T(8,128)(2,1)S(1)}, u32[]{:S(2)}, u32[]{:S(2)}) collective-permute-start(bf16[24,4096]{1,0:T(8,128)(2,1)S(1)} %fusion.107), channel_id=1, source_target_pairs={{0,4},{4,8},{8,12},{1,5},{5,9},{9,13},{2,6},{6,10},{10,14},{3,7},{... | collective-permute-start | bytes 589832 | tf_op jit(solution)/shard_map/while/body/eval_jaxpr/ppermute | solution.py:16
  222.2 0.6 copy-start.5
  222.2 0.6 copy-start.6
  222.2 0.6 copy-start.7
Sparse Core Ops, SparseCore 0:
  51.3 21.1 all-gather.6
  98.5 20.6 all-gather.6
  145.2 20.6 all-gather.6
  191.9 20.6 all-gather.6
